TPU v7x, 512 devices: a whole 4x4x16 slice. The times are simulated.
512 devices in a mesh: dp: 32 (over z, x_lo), fsdp: 16 (over y, x_hi, core).
Axes of the slice: x: 4 (x_hi: 2, x_lo: 2; x = x_hi * 2 + x_lo), y: 4, z: 16, core: 2. Of those that a mesh axis runs over, the one named last changes fastest.
Arguments:
- images: bfloat16 [1024, 8, 8, 3072], P(('dp', 'fsdp')), may hold values from -6 to 6
- dw_weight: float32 [49, 3072], P(None, 'fsdp'), may hold values from -0.875 to 0.875
- dw_bias: float32 [3072], P('fsdp'), may hold values from -1 to 1
- block_gain: float32 [3072], P('fsdp'), may hold values from 0.5 to 1.5
- head_gain: float32 [3072], P('fsdp'), may hold values from 0.5 to 1.5
- projection: bfloat16 [3072, 512], P('fsdp'), may hold values from -0.109375 to 0.109375
- text: bfloat16 [1024, 512], P(('dp', 'fsdp')), may hold values from -6 to 6
Outputs:
- loss: float32 [], replicated
- grad_images: bfloat16 [1024, 8, 8, 3072], P(('dp', 'fsdp'))
- grad_dw_weight: float32 [49, 3072], P(None, 'fsdp')
- grad_dw_bias: float32 [3072], P('fsdp')
- grad_block_gain: float32 [3072], P('fsdp')
- grad_head_gain: float32 [3072], P('fsdp')
- grad_projection: float32 [3072, 512], P('fsdp')
- grad_text: float32 [1024, 512], P(('dp', 'fsdp'))
All inputs are finite; a program needn't handle non-finite values.
Results may differ from a plain program's by a relative error of at most 0.012.
Values may be sent and summed in bfloat16 or wider, within the bound.
A program may use at most 64 MiB of HBM per device.

v0:
```python
import jax
import jax.numpy as jnp
from jax import lax
from jax.sharding import PartitionSpec as P

KERNEL = 7
MAP_SIDE = 8
LOGIT_SCALE = 14.0
EPSILON = 1e-06


def depthwise(padded, weight):
    total = jnp.zeros(padded.shape[:1] + (MAP_SIDE, MAP_SIDE, padded.shape[3]), jnp.float32)
    for tap_row in range(KERNEL):
        for tap_col in range(KERNEL):
            window = padded[:, tap_row : tap_row + MAP_SIDE, tap_col : tap_col + MAP_SIDE, :]
            total = total + window * weight[tap_row * KERNEL + tap_col]
    return total


def contract(left, right, left_dim, right_dim):
    return lax.dot_general(
        left, right, (((left_dim,), (right_dim,)), ((), ())), preferred_element_type=jnp.float32
    )


def local(images, dw_weight, dw_bias, block_gain, head_gain, projection, text):
    full_weight, full_bias, full_block, full_head = (
        lax.all_gather(dw_weight, "fsdp", axis=1, tiled=True),
        lax.all_gather(dw_bias, "fsdp", axis=0, tiled=True),
        lax.all_gather(block_gain, "fsdp", axis=0, tiled=True),
        lax.all_gather(head_gain, "fsdp", axis=0, tiled=True),
    )
    margin = KERNEL // 2
    as_float = images.astype(jnp.float32)
    padded = jnp.pad(as_float, ((0, 0), (margin, margin), (margin, margin), (0, 0)))
    conv_out = depthwise(padded, full_weight) + full_bias
    centred = conv_out - jnp.mean(conv_out, axis=3, keepdims=True)
    inverse = lax.rsqrt(jnp.mean(centred * centred, axis=3, keepdims=True) + EPSILON)
    normal_z = centred * inverse
    hidden = as_float + normal_z * full_block
    pooled = jnp.mean(hidden, axis=(1, 2))
    pool_centred = pooled - jnp.mean(pooled, axis=1, keepdims=True)
    pool_inverse = lax.rsqrt(jnp.mean(pool_centred * pool_centred, axis=1, keepdims=True) + EPSILON)
    pool_normed = pool_centred * pool_inverse
    query = (pool_normed * full_head).astype(jnp.bfloat16)
    query_parts = lax.all_to_all(query, "fsdp", split_axis=1, concat_axis=0, tiled=True)
    panels = lax.all_gather(projection, "fsdp", axis=0, tiled=True)
    embedding = jnp.dot(query, panels, preferred_element_type=jnp.float32)
    image_scale = lax.rsqrt(jnp.sum(embedding * embedding, axis=1, keepdims=True) + EPSILON)
    image_f = embedding * image_scale
    image_unit = image_f.astype(jnp.bfloat16)
    text_float = text.astype(jnp.float32)
    text_scale = lax.rsqrt(jnp.sum(text_float * text_float, axis=1, keepdims=True) + EPSILON)
    text_f = text_float * text_scale
    text_unit = text_f.astype(jnp.bfloat16)
    image_all, text_all = (
        lax.all_gather(image_unit, ("dp", "fsdp"), axis=0, tiled=True),
        lax.all_gather(text_unit, ("dp", "fsdp"), axis=0, tiled=True),
    )
    local_count = images.shape[0]
    offset = lax.axis_index(("dp", "fsdp")) * local_count
    row_logits = LOGIT_SCALE * contract(image_unit, text_all, 1, 1)
    col_logits = LOGIT_SCALE * contract(image_all, text_unit, 1, 1)
    row_lse = jnp.log(jnp.sum(jnp.exp(row_logits), axis=1))
    col_lse = jnp.log(jnp.sum(jnp.exp(col_logits), axis=0))
    diagonal = LOGIT_SCALE * jnp.sum(
        image_unit.astype(jnp.float32) * text_unit.astype(jnp.float32), axis=1
    )
    every_row, every_col, every_diag = (
        lax.all_gather(row_lse, ("dp", "fsdp"), axis=0, tiled=True),
        lax.all_gather(col_lse, ("dp", "fsdp"), axis=0, tiled=True),
        lax.all_gather(diagonal, ("dp", "fsdp"), axis=0, tiled=True),
    )
    total_pairs = every_row.shape[0]
    loss = (jnp.sum(every_row) + jnp.sum(every_col) - 2.0 * jnp.sum(every_diag)) / (
        2.0 * total_pairs
    )
    positions = jnp.arange(total_pairs, dtype=jnp.int32)
    owners = offset + jnp.arange(local_count, dtype=jnp.int32)
    onehot = (positions[None, :] == owners[:, None]).astype(jnp.float32)
    row_weights = (
        jnp.exp(row_logits - row_lse[:, None])
        + jnp.exp(row_logits - every_col[None, :])
        - 2.0 * onehot
    ).astype(jnp.bfloat16)
    col_weights = (
        jnp.exp(col_logits - every_row[:, None])
        + jnp.exp(col_logits - col_lse[None, :])
        - 2.0 * onehot.T
    ).astype(jnp.bfloat16)
    d_image = 7.0 * jnp.dot(row_weights, text_all, preferred_element_type=jnp.float32)
    d_caption = 7.0 * contract(col_weights, image_all, 0, 0)
    d_embedding = (
        image_scale * (d_image - image_f * jnp.sum(image_f * d_image, axis=1, keepdims=True))
    ).astype(jnp.bfloat16)
    grad_text = text_scale * (
        d_caption - text_f * jnp.sum(text_f * d_caption, axis=1, keepdims=True)
    )
    demb_group = lax.all_gather(d_embedding, "fsdp", axis=0, tiled=True)
    proj_grad = contract(query_parts, demb_group, 0, 0)
    d_query = contract(d_embedding, panels, 1, 1)
    d_normed = d_query * full_head
    g_head = jnp.sum(d_query * pool_normed, axis=0)
    d_pooled = pool_inverse * (
        d_normed
        - jnp.mean(d_normed, axis=1, keepdims=True)
        - pool_normed * jnp.mean(d_normed * pool_normed, axis=1, keepdims=True)
    )
    d_hidden = (d_pooled / float(MAP_SIDE * MAP_SIDE))[:, None, None, :]
    d_norm = d_hidden * full_block
    g_block = jnp.sum(d_hidden * normal_z, axis=(0, 1, 2))
    d_conv = inverse * (
        d_norm
        - jnp.mean(d_norm, axis=3, keepdims=True)
        - normal_z * jnp.mean(d_norm * normal_z, axis=3, keepdims=True)
    )
    g_bias = jnp.sum(d_conv, axis=(0, 1, 2))
    d_padded = jnp.pad(d_conv, ((0, 0), (margin, margin), (margin, margin), (0, 0)))
    tap_grads = []
    d_images = d_hidden + jnp.zeros_like(d_conv)
    for tap_row in range(KERNEL):
        for tap_col in range(KERNEL):
            window = padded[:, tap_row : tap_row + MAP_SIDE, tap_col : tap_col + MAP_SIDE, :]
            tap_grads.append(jnp.sum(d_conv * window, axis=(0, 1, 2)))
            back = d_padded[
                :,
                2 * margin - tap_row : 2 * margin - tap_row + MAP_SIDE,
                2 * margin - tap_col : 2 * margin - tap_col + MAP_SIDE,
                :,
            ]
            d_images = d_images + back * full_weight[tap_row * KERNEL + tap_col]
    g_weight = jnp.stack(tap_grads)
    part_weight, part_bias, part_block, part_head = (
        lax.psum_scatter(g_weight, "fsdp", scatter_dimension=1, tiled=True),
        lax.psum_scatter(g_bias, "fsdp", scatter_dimension=0, tiled=True),
        lax.psum_scatter(g_block, "fsdp", scatter_dimension=0, tiled=True),
        lax.psum_scatter(g_head, "fsdp", scatter_dimension=0, tiled=True),
    )
    sum_weight, sum_bias, sum_block, sum_head, sum_proj = lax.psum(
        (part_weight, part_bias, part_block, part_head, proj_grad), "dp"
    )
    return (
        loss,
        d_images.astype(jnp.bfloat16),
        sum_weight,
        sum_bias,
        sum_block,
        sum_head,
        sum_proj,
        grad_text,
    )


def solution(mesh):
    return jax.shard_map(
        local,
        mesh=mesh,
        in_specs=(
            P(("dp", "fsdp"), None, None, None),
            P(None, "fsdp"),
            P("fsdp"),
            P("fsdp"),
            P("fsdp"),
            P("fsdp", None),
            P(("dp", "fsdp"), None),
        ),
        out_specs=(
            P(),
            P(("dp", "fsdp"), None, None, None),
            P(None, "fsdp"),
            P("fsdp"),
            P("fsdp"),
            P("fsdp"),
            P("fsdp", None),
            P(("dp", "fsdp"), None),
        ),
        check_vma=False,
    )
```

profile of v0, /device:TPU:4, one launch (start us, length us, event | category | flops | bytes accessed | tf_op | source)
XLA Modules:
  0.0 2228.4 jit_solution(11575561516436154558)
XLA Ops:
  8.0 28.4 %all-gather = f32[16,192,49]{1,2,0:T(8,128)S(1)} all-gather(f32[1,192,49]{1,2,0:T(8,128)} %bitcast.227), channel_id=1, replica_groups=mesh['dp'=32,'fsdp'=16] {'fsdp'}, dimensions={0}, use_global_device_ids=true | all-gather | bytes 639744 | tf_op jit(solution)/shard_map/all_gather | solution.py:29
  40.2 62.7 %all-reduce.14 = (f32[3072]{0:T(1024)}, f32[3072]{0:T(1024)}, f32[3072]{0:T(1024)S(1)}) all-reduce(f32[3072]{0:T(1024)S(1)} %dynamic-update-slice, f32[3072]{0:T(1024)S(1)} %dynamic-update-slice.1, f32[3072]{0:T(1024)S(1)} %dynamic-update-slice.2), channel_id=1, replica_groups=mesh['dp'=32,'fsdp'=16] {'fsdp'}, use_global_device_ids=true, to_apply=%add.2 | all-reduce | flops 9216 | bytes 73728
  103.7 14.5 fusion.131
  121.1 2.6 multiply_reduce_fusion.58
  128.6 9.2 all-to-all-start
  140.3 2.3 all-to-all-done
  144.0 749.1 %all-gather.12.cloned.1.call-done = bf16[512,2,512]{2,1,0:T(2,128)(2,1)} async-done(((bf16[1,2,512]{2,1,0:T(2,128)(2,1)}), bf16[512,2,512]{2,1,0:T(2,128)(2,1)}) %all-gather.12.cloned.1.call-update) | async-done | bytes 1048592 | tf_op jit(solution)/shard_map/all_gather | solution.py:58
  893.1 2.3 reshape.185
  895.3 2.3 exponential_reduce_fusion
  897.7 756.2 %all-gather.10.cloned.1.call-done = bf16[512,2,512]{2,1,0:T(2,128)(2,1)} async-done(((bf16[1,2,512]{2,1,0:T(2,128)(2,1)}), bf16[512,2,512]{2,1,0:T(2,128)(2,1)}) %all-gather.10.cloned.1.call-update) | async-done | bytes 1048592 | tf_op jit(solution)/shard_map/all_gather | solution.py:59
  1653.8 2.3 reshape.183
  1656.1 1.7 exponential_reduce_fusion.1
  1658.9 101.7 %all-reduce.11 = (f32[1024]{0:T(1024)}, f32[1024]{0:T(1024)S(1)}, f32[1024]{0:T(1024)}) all-reduce(f32[1024]{0:T(1024)S(1)} %get-tuple-element.153, f32[1024]{0:T(1024)S(1)} %get-tuple-element.151, f32[1024]{0:T(1024)S(1)} %multiply_dynamic-update-slice_fusion), channel_id=1, replica_groups=mesh['dp'=32,'fsdp'=16] {'dp','fsdp'}, use_global_device_ids=true, to_apply=%add.5 | all-reduce | flops 3072 | bytes 24576
  1763.1 3.4 multiply_reduce_fusion.52
  1767.9 4.7 multiply_reduce_fusion.1
  1772.6 2.4 fusion.128
  1775.2 3.8 multiply_reduce_fusion.19
  1779.1 21.1 all-gather.3
  1800.2 62.4 %all-reduce.13 = (f32[3072]{0:T(1024)S(1)}, f32[3072]{0:T(1024)S(1)}, f32[3072]{0:T(1024)S(1)}) all-reduce(f32[3072]{0:T(1024)S(1)} %get-tuple-element.58, f32[3072]{0:T(1024)S(1)} %copy-done.73, f32[3072]{0:T(1024)S(1)} %copy-done.72), channel_id=3, replica_groups=mesh['dp'=32,'fsdp'=16] {'fsdp'}, use_global_device_ids=true, to_apply=%region_70.71.clone | all-reduce | flops 9216 | bytes 73728
  1868.6 9.5 fusion.97
  1882.4 70.2 %reduce-scatter.4.cloned.1.call-done = f32[192,49]{1,0:T(8,128)} async-done(((f32[3072,49]{1,0:T(8,128)}), f32[192,49]{1,0:T(8,128)}) %reduce-scatter.4.cloned.1.call-update) | async-done | bytes 37648
  1953.7 123.0 %all-reduce.12 = (f32[49,192]{1,0:T(8,128)}, f32[192]{0:T(256)}, f32[192]{0:T(256)}, f32[192]{0:T(256)}) all-reduce(f32[49,192]{1,0:T(8,128)S(1)} %copy.24, f32[192]{0:T(256)S(1)} %dynamic-slice.4, f32[192]{0:T(256)S(1)} %dynamic-slice.6, f32[192]{0:T(256)S(1)} %dynamic-slice.8), channel_id=1, replica_groups=mesh['dp'=32,'fsdp'=16] {'dp'}, use_global_device_ids=true, to_apply=%region_68.69 | all-reduce | flops 9984 | bytes 79872 | tf_op jit(solution)/shard_map/psum | solution.py:140
  2076.7 142.3 %all-reduce.17.cloned.1.call-done = f32[192,512]{1,0:T(8,128)} async-done(((f32[192,512]{1,0:T(8,128)}), f32[192,512]{1,0:T(8,128)}) %all-reduce.17.cloned.1.call-update) | async-done | bytes 393232 | tf_op jit(solution)/shard_map/psum | solution.py:140
  2219.0 1.8 copy.35
  (263 shorter events, 28.9 us)
Async XLA Ops:
  7.2 113.9 %all-gather.8.cloned.1.call-start = ((), (), s32[]{:S(2)}) async-start(), calls=%async_computation.2 | async-start | bytes 3342336 | tf_op jit(solution)/shard_map/all_gather | solution.py:48
  7.9 885.2 %all-gather.12.cloned.1.call-start = ((), (), s32[]{:S(2)}) async-start(), calls=%async_computation.5 | async-start | bytes 1050624 | tf_op jit(solution)/shard_map/all_gather | solution.py:58
  125.0 1528.8 %all-gather.10.cloned.1.call-start = ((), (), s32[]{:S(2)}) async-start(), calls=%async_computation.4 | async-start | bytes 1050624 | tf_op jit(solution)/shard_map/all_gather | solution.py:59
  128.0 767.3 %copy-start.76 = (bf16[2,512]{1,0:T(2,128)(2,1)S(1)}, bf16[2,512]{1,0:T(2,128)(2,1)}, u32[]{:S(2)}) copy-start(bf16[2,512]{1,0:T(2,128)(2,1)} %get-tuple-element.93) | copy-start | bytes 6148
  128.6 14.0 all-to-all-start
  137.8 1814.9 %reduce-scatter.4.cloned.1.call-start = ((), (), s32[]{:S(2)}) async-start(), calls=%async_computation.6 | async-start | bytes 1671168
  895.3 760.8 %copy-start.75 = (bf16[2,512]{1,0:T(2,128)(2,1)S(1)}, bf16[2,512]{1,0:T(2,128)(2,1)}, u32[]{:S(2)}) copy-start(bf16[2,512]{1,0:T(2,128)(2,1)} %get-tuple-element.94) | copy-start | bytes 6148
  1656.1 107.0 %copy-start.80 = (f32[2]{0:T(128)S(1)}, f32[2]{0:T(128)}, u32[]{:S(2)}) copy-start(f32[2]{0:T(128)} %copy-done.79) | copy-start | bytes 28
  1656.1 107.0 %copy-start.83 = (f32[2]{0:T(128)S(1)}, f32[2]{0:T(128)}, u32[]{:S(2)}) copy-start(f32[2]{0:T(128)} %copy-done.82) | copy-start | bytes 28
  1775.1 87.8 %copy-start.54 = (f32[3072]{0:T(1024)S(1)}, f32[3072]{0:T(1024)}, u32[]{:S(2)}) copy-start(f32[3072]{0:T(1024)} %get-tuple-element.9) | copy-start | bytes 36868
  1775.1 87.8 %copy-start.55 = (f32[3072]{0:T(1024)S(1)}, f32[3072]{0:T(1024)}, u32[]{:S(2)}) copy-start(f32[3072]{0:T(1024)} %get-tuple-element.10) | copy-start | bytes 36868
  1775.1 87.8 %copy-start.56 = (f32[3072]{0:T(1024)S(1)}, f32[3072]{0:T(1024)}, u32[]{:S(2)}) copy-start(f32[3072]{0:T(1024)} %get-tuple-element.11) | copy-start | bytes 36868
  1775.1 87.8 %copy-start.57 = (f32[3072]{0:T(1024)S(1)}, f32[3072]{0:T(1024)}, u32[]{:S(2)}) copy-start(f32[3072]{0:T(1024)} %get-tuple-element.12) | copy-start | bytes 36868
  1775.1 87.8 %copy-start.58 = (f32[3072]{0:T(1024)S(1)}, f32[3072]{0:T(1024)}, u32[]{:S(2)}) copy-start(f32[3072]{0:T(1024)} %get-tuple-element.13) | copy-start | bytes 36868
  1775.1 87.8 %copy-start.59 = (f32[3072]{0:T(1024)S(1)}, f32[3072]{0:T(1024)}, u32[]{:S(2)}) copy-start(f32[3072]{0:T(1024)} %get-tuple-element.14) | copy-start | bytes 36868
  1775.1 87.8 %copy-start.60 = (f32[3072]{0:T(1024)S(1)}, f32[3072]{0:T(1024)}, u32[]{:S(2)}) copy-start(f32[3072]{0:T(1024)} %get-tuple-element.15) | copy-start | bytes 36868
  1775.1 87.8 %copy-start.61 = (f32[3072]{0:T(1024)S(1)}, f32[3072]{0:T(1024)}, u32[]{:S(2)}) copy-start(f32[3072]{0:T(1024)} %get-tuple-element.16) | copy-start | bytes 36868
  1775.1 87.8 %copy-start.62 = (f32[3072]{0:T(1024)S(1)}, f32[3072]{0:T(1024)}, u32[]{:S(2)}) copy-start(f32[3072]{0:T(1024)} %get-tuple-element.17) | copy-start | bytes 36868
  1775.1 87.8 %copy-start.63 = (f32[3072]{0:T(1024)S(1)}, f32[3072]{0:T(1024)}, u32[]{:S(2)}) copy-start(f32[3072]{0:T(1024)} %get-tuple-element.18) | copy-start | bytes 36868
  1775.2 87.8 %copy-start.64 = (f32[3072]{0:T(1024)S(1)}, f32[3072]{0:T(1024)}, u32[]{:S(2)}) copy-start(f32[3072]{0:T(1024)} %get-tuple-element.19) | copy-start | bytes 36868
  1775.2 87.8 %copy-start.65 = (f32[3072]{0:T(1024)S(1)}, f32[3072]{0:T(1024)}, u32[]{:S(2)}) copy-start(f32[3072]{0:T(1024)} %get-tuple-element.20) | copy-start | bytes 36868
  1775.2 87.8 %copy-start.66 = (f32[3072]{0:T(1024)S(1)}, f32[3072]{0:T(1024)}, u32[]{:S(2)}) copy-start(f32[3072]{0:T(1024)} %get-tuple-element.21) | copy-start | bytes 36868
  1775.2 87.8 %copy-start.67 = (f32[3072]{0:T(1024)S(1)}, f32[3072]{0:T(1024)}, u32[]{:S(2)}) copy-start(f32[3072]{0:T(1024)} %get-tuple-element.22) | copy-start | bytes 36868
  1865.8 353.2 %all-reduce.17.cloned.1.call-start = ((), (), s32[]{:S(2)}) async-start(), calls=%async_computation.3 | async-start | bytes 786432 | tf_op jit(solution)/shard_map/psum | solution.py:140
  (78 other events, 984.4 us)
Sparse Core Ops, SparseCore 0:
  11.3 68.0 all-gather.7
  125.1 767.9 all-gather.11
  895.8 758.0 all-gather.9
  1865.9 86.6 reduce-scatter.3
  1956.0 262.9 all-reduce.16
where the time goes:
time: 2230 us
  waiting for transfers between devices  1720 us (77%)
  blocking collectives  399 us (18%)
  other arithmetic  47 us (2%)
    all_gather x1, waiting for transfers between devices, local(): lax.all_gather(text_unit, ('dp', 'fsdp'), axis=0, tiled=True)  756 us
    all_gather x1, waiting for transfers between devices, local(): lax.all_gather(image_unit, ('dp', 'fsdp'), axis=0, tiled=True)  749 us
    unnamed x3, blocking collectives  227 us
    psum x1, waiting for transfers between devices, local(): lax.psum((part_weight, part_bias, part_block, part_head, proj_grad), 'dp')  142 us
    psum x1, blocking collectives, local(): lax.psum((part_weight, part_bias, part_block, part_head, proj_grad), 'dp')  123 us
    unnamed x6, waiting for transfers between devices  71.6 us
  transfers between devices with their start and end apart: 6, of which 5 were waited for; matrix products, arithmetic and copies ran while one was open for 2% of the time, Pallas kernels for 0%

commit v1 on v0

--- a/solution.py
+++ b/solution.py
@@ -55,7 +55,12 @@
     text_f = text_float * text_scale
     text_unit = text_f.astype(jnp.bfloat16)
     image_all, text_all = (
-        lax.all_gather(image_unit, ("dp", "fsdp"), axis=0, tiled=True),
+        jnp.concatenate(
+            lax.all_to_all(
+                jnp.stack([image_unit] * lax.axis_size(("dp", "fsdp"))), ("dp", "fsdp"), 0, 0
+            ),
+            axis=0,
+        ),
         lax.all_gather(text_unit, ("dp", "fsdp"), axis=0, tiled=True),
     )
     local_count = images.shape[0]

time: 2230 us -> 1510 us (0.68)
  waiting for transfers between devices: 1720 us -> 983 us
  starting transfers between devices: 9.36 us -> 32 us
    all_gather x1 -> x0, waiting for transfers between devices: 749 us -> none  [local(): lax.all_gather(image_unit, ('dp', 'fsdp'), axis=0, tiled=True)]
    all_to_all x0 -> x1, starting transfers between devices: none -> 22.7 us  [local(): lax.all_to_all(jnp.stack([image_unit] * lax.axis_size(('dp', 'fsdp'))), (...]
    unnamed x6 -> x5, waiting for transfers between devices: 71.6 us -> 71.8 us
  transfers between devices with their start and end apart: 6 -> 6, of which waited for: 5 -> 4; matrix products, arithmetic and copies ran while one was open for 2% -> 3% of each run, Pallas kernels for 0% -> 0%
where the time goes in v1:
time: 1510 us
  waiting for transfers between devices  983 us (65%)
  blocking collectives  399 us (26%)
  other arithmetic  47.6 us (3%)
  starting transfers between devices  32 us (2%)
  local copies, waits for them, and re-layouts  20 us (1%)
  between operations  19.5 us (1%)
    all_gather x1, waiting for transfers between devices, local(): lax.all_gather(text_unit, ('dp', 'fsdp'), axis=0, tiled=True)  768 us
    unnamed x3, blocking collectives  227 us
    psum x1, waiting for transfers between devices, local(): lax.psum((part_weight, part_bias, part_block, part_head, proj_grad), 'dp')  142 us
    psum x1, blocking collectives, local(): lax.psum((part_weight, part_bias, part_block, part_head, proj_grad), 'dp')  123 us
    unnamed x5, waiting for transfers between devices  71.8 us
  transfers between devices with their start and end apart: 6, of which 4 were waited for; matrix products, arithmetic and copies ran while one was open for 3% of the time, Pallas kernels for 0%

profile of v1, /device:TPU:4, one launch (start us, length us, event | category | flops | bytes accessed | tf_op | source)
XLA Modules:
  0.0 1514.1 jit_solution(13739329893725585453)
XLA Ops:
  7.9 28.4 %all-gather = f32[16,192,49]{1,2,0:T(8,128)S(1)} all-gather(f32[1,192,49]{1,2,0:T(8,128)} %bitcast.226), channel_id=1, replica_groups=mesh['dp'=32,'fsdp'=16] {'fsdp'}, dimensions={0}, use_global_device_ids=true | all-gather | bytes 639744 | tf_op jit(solution)/shard_map/all_gather | solution.py:29
  40.0 62.8 %all-reduce.14 = (f32[3072]{0:T(1024)}, f32[3072]{0:T(1024)}, f32[3072]{0:T(1024)S(1)}) all-reduce(f32[3072]{0:T(1024)S(1)} %dynamic-update-slice, f32[3072]{0:T(1024)S(1)} %dynamic-update-slice.1, f32[3072]{0:T(1024)S(1)} %dynamic-update-slice.2), channel_id=1, replica_groups=mesh['dp'=32,'fsdp'=16] {'fsdp'}, use_global_device_ids=true, to_apply=%add.2 | all-reduce | flops 9216 | bytes 73728
  103.5 14.5 fusion.131
  124.9 9.2 all-to-all-start.1
  134.2 2.6 multiply_reduce_fusion.58
  140.4 22.7 %all-to-all-start = ((bf16[512,2,512]{2,1,0:T(2,128)(2,1)}), bf16[512,2,512]{2,1,0:T(2,128)(2,1)}, u32[]{:S(2)}, u32[]{:S(2)}) async-start(bf16[512,2,512]{2,1,0:T(2,128)(2,1)} %stack.102), calls=%async_computation | async-start | bytes 2097152 | tf_op jit(solution)/shard_map/all_to_all | solution.py:59
  167.1 767.8 %all-gather.8.cloned.1.call-done = bf16[512,2,512]{2,1,0:T(2,128)(2,1)} async-done(((bf16[1,2,512]{2,1,0:T(2,128)(2,1)}), bf16[512,2,512]{2,1,0:T(2,128)(2,1)}) %all-gather.8.cloned.1.call-update) | async-done | bytes 1048592 | tf_op jit(solution)/shard_map/all_gather | solution.py:64
  934.9 2.3 reshape.189
  937.1 1.7 exponential_reduce_fusion.1
  939.4 2.3 reshape.170
  941.7 2.3 exponential_reduce_fusion
  944.6 101.5 %all-reduce.11 = (f32[1024]{0:T(1024)}, f32[1024]{0:T(1024)S(1)}, f32[1024]{0:T(1024)}) all-reduce(f32[1024]{0:T(1024)S(1)} %get-tuple-element.153, f32[1024]{0:T(1024)S(1)} %get-tuple-element.151, f32[1024]{0:T(1024)S(1)} %multiply_dynamic-update-slice_fusion), channel_id=1, replica_groups=mesh['dp'=32,'fsdp'=16] {'dp','fsdp'}, use_global_device_ids=true, to_apply=%add.5 | all-reduce | flops 3072 | bytes 24576
  1048.6 3.4 multiply_reduce_fusion.52
  1053.4 4.7 multiply_reduce_fusion.1
  1058.1 2.4 fusion.128
  1060.7 3.8 multiply_reduce_fusion.19
  1064.6 21.1 %all-gather.2 = bf16[16,2,512]{2,1,0:T(2,128)(2,1)S(1)} all-gather(bf16[1,2,512]{2,1,0:T(2,128)(2,1)S(1)} %bitcast.276), channel_id=1, replica_groups=mesh['dp'=32,'fsdp'=16] {'fsdp'}, dimensions={0}, use_global_device_ids=true | all-gather | bytes 34816 | tf_op jit(solution)/shard_map/all_gather | solution.py:105
  1085.7 62.4 %all-reduce.13 = (f32[3072]{0:T(1024)S(1)}, f32[3072]{0:T(1024)S(1)}, f32[3072]{0:T(1024)S(1)}) all-reduce(f32[3072]{0:T(1024)S(1)} %get-tuple-element.58, f32[3072]{0:T(1024)S(1)} %copy-done.74, f32[3072]{0:T(1024)S(1)} %copy-done.73), channel_id=3, replica_groups=mesh['dp'=32,'fsdp'=16] {'fsdp'}, use_global_device_ids=true, to_apply=%region_70.71.clone | all-reduce | flops 9216 | bytes 73728
  1149.4 1.7 copy.23
  1154.1 9.5 fusion.97
  1167.9 70.4 %reduce-scatter.4.cloned.1.call-done = f32[192,49]{1,0:T(8,128)} async-done(((f32[3072,49]{1,0:T(8,128)}), f32[192,49]{1,0:T(8,128)}) %reduce-scatter.4.cloned.1.call-update) | async-done | bytes 37648
  1239.3 123.1 %all-reduce.12 = (f32[49,192]{1,0:T(8,128)}, f32[192]{0:T(256)}, f32[192]{0:T(256)}, f32[192]{0:T(256)}) all-reduce(f32[49,192]{1,0:T(8,128)S(1)} %copy.24, f32[192]{0:T(256)S(1)} %dynamic-slice.4, f32[192]{0:T(256)S(1)} %dynamic-slice.6, f32[192]{0:T(256)S(1)} %dynamic-slice.8), channel_id=1, replica_groups=mesh['dp'=32,'fsdp'=16] {'dp'}, use_global_device_ids=true, to_apply=%region_68.69 | all-reduce | flops 9984 | bytes 79872 | tf_op jit(solution)/shard_map/psum | solution.py:145
  1362.4 142.3 %all-reduce.17.cloned.1.call-done = f32[192,512]{1,0:T(8,128)} async-done(((f32[192,512]{1,0:T(8,128)}), f32[192,512]{1,0:T(8,128)}) %all-reduce.17.cloned.1.call-update) | async-done | bytes 393232 | tf_op jit(solution)/shard_map/psum | solution.py:145
  1504.6 1.8 copy.35
  (265 shorter events, 29.9 us)
Async XLA Ops:
  7.2 127.1 %all-gather.6.cloned.1.call-start = ((), (), s32[]{:S(2)}) async-start(), calls=%async_computation.3 | async-start | bytes 3342336 | tf_op jit(solution)/shard_map/all_gather | solution.py:48
  124.9 14.0 all-to-all-start.1
  140.4 799.1 %all-to-all-start = ((bf16[512,2,512]{2,1,0:T(2,128)(2,1)}), bf16[512,2,512]{2,1,0:T(2,128)(2,1)}, u32[]{:S(2)}, u32[]{:S(2)}) async-start(bf16[512,2,512]{2,1,0:T(2,128)(2,1)} %stack.102), calls=%async_computation | async-start | bytes 2097152 | tf_op jit(solution)/shard_map/all_to_all | solution.py:59
  163.1 771.8 %all-gather.8.cloned.1.call-start = ((), (), s32[]{:S(2)}) async-start(), calls=%async_computation.5 | async-start | bytes 1050624 | tf_op jit(solution)/shard_map/all_gather | solution.py:64
  163.8 1074.5 %reduce-scatter.4.cloned.1.call-start = ((), (), s32[]{:S(2)}) async-start(), calls=%async_computation.6 | async-start | bytes 1671168
  941.7 106.8 %copy-start.81 = (f32[2]{0:T(128)S(1)}, f32[2]{0:T(128)}, u32[]{:S(2)}) copy-start(f32[2]{0:T(128)} %copy-done.80) | copy-start | bytes 28
  941.7 106.8 %copy-start.84 = (f32[2]{0:T(128)S(1)}, f32[2]{0:T(128)}, u32[]{:S(2)}) copy-start(f32[2]{0:T(128)} %copy-done.83) | copy-start | bytes 28
  1060.5 87.8 %copy-start.54 = (f32[3072]{0:T(1024)S(1)}, f32[3072]{0:T(1024)}, u32[]{:S(2)}) copy-start(f32[3072]{0:T(1024)} %get-tuple-element.9) | copy-start | bytes 36868
  1060.6 87.8 %copy-start.55 = (f32[3072]{0:T(1024)S(1)}, f32[3072]{0:T(1024)}, u32[]{:S(2)}) copy-start(f32[3072]{0:T(1024)} %get-tuple-element.10) | copy-start | bytes 36868
  1060.6 87.8 %copy-start.56 = (f32[3072]{0:T(1024)S(1)}, f32[3072]{0:T(1024)}, u32[]{:S(2)}) copy-start(f32[3072]{0:T(1024)} %get-tuple-element.11) | copy-start | bytes 36868
  1060.6 87.8 %copy-start.57 = (f32[3072]{0:T(1024)S(1)}, f32[3072]{0:T(1024)}, u32[]{:S(2)}) copy-start(f32[3072]{0:T(1024)} %get-tuple-element.12) | copy-start | bytes 36868
  1060.6 87.8 %copy-start.58 = (f32[3072]{0:T(1024)S(1)}, f32[3072]{0:T(1024)}, u32[]{:S(2)}) copy-start(f32[3072]{0:T(1024)} %get-tuple-element.13) | copy-start | bytes 36868
  1060.6 87.8 %copy-start.59 = (f32[3072]{0:T(1024)S(1)}, f32[3072]{0:T(1024)}, u32[]{:S(2)}) copy-start(f32[3072]{0:T(1024)} %get-tuple-element.14) | copy-start | bytes 36868
  1060.6 87.8 %copy-start.60 = (f32[3072]{0:T(1024)S(1)}, f32[3072]{0:T(1024)}, u32[]{:S(2)}) copy-start(f32[3072]{0:T(1024)} %get-tuple-element.15) | copy-start | bytes 36868
  1060.6 87.8 %copy-start.61 = (f32[3072]{0:T(1024)S(1)}, f32[3072]{0:T(1024)}, u32[]{:S(2)}) copy-start(f32[3072]{0:T(1024)} %get-tuple-element.16) | copy-start | bytes 36868
  1060.6 87.8 %copy-start.62 = (f32[3072]{0:T(1024)S(1)}, f32[3072]{0:T(1024)}, u32[]{:S(2)}) copy-start(f32[3072]{0:T(1024)} %get-tuple-element.17) | copy-start | bytes 36868
  1060.6 87.8 %copy-start.63 = (f32[3072]{0:T(1024)S(1)}, f32[3072]{0:T(1024)}, u32[]{:S(2)}) copy-start(f32[3072]{0:T(1024)} %get-tuple-element.18) | copy-start | bytes 36868
  1060.6 87.8 %copy-start.64 = (f32[3072]{0:T(1024)S(1)}, f32[3072]{0:T(1024)}, u32[]{:S(2)}) copy-start(f32[3072]{0:T(1024)} %get-tuple-element.19) | copy-start | bytes 36868
  1060.7 87.8 %copy-start.65 = (f32[3072]{0:T(1024)S(1)}, f32[3072]{0:T(1024)}, u32[]{:S(2)}) copy-start(f32[3072]{0:T(1024)} %get-tuple-element.20) | copy-start | bytes 36868
  1060.7 87.8 %copy-start.66 = (f32[3072]{0:T(1024)S(1)}, f32[3072]{0:T(1024)}, u32[]{:S(2)}) copy-start(f32[3072]{0:T(1024)} %get-tuple-element.21) | copy-start | bytes 36868
  1060.7 87.8 %copy-start.67 = (f32[3072]{0:T(1024)S(1)}, f32[3072]{0:T(1024)}, u32[]{:S(2)}) copy-start(f32[3072]{0:T(1024)} %get-tuple-element.22) | copy-start | bytes 36868
  1060.7 87.8 %copy-start.68 = (f32[3072]{0:T(1024)S(1)}, f32[3072]{0:T(1024)}, u32[]{:S(2)}) copy-start(f32[3072]{0:T(1024)} %get-tuple-element.23) | copy-start | bytes 36868
  1060.7 87.8 %copy-start.69 = (f32[3072]{0:T(1024)S(1)}, f32[3072]{0:T(1024)}, u32[]{:S(2)}) copy-start(f32[3072]{0:T(1024)} %get-tuple-element.24) | copy-start | bytes 36868
  1151.3 353.3 %all-reduce.17.cloned.1.call-start = ((), (), s32[]{:S(2)}) async-start(), calls=%async_computation.4 | async-start | bytes 786432 | tf_op jit(solution)/shard_map/psum | solution.py:145
  (79 other events, 788.0 us)
Sparse Core Ops, SparseCore 0:
  11.3 68.0 all-gather.5
  166.6 768.2 all-gather.7
  1151.4 86.8 reduce-scatter.3
  1241.7 262.9 all-reduce.16
